TPU v7x, 256 devices: a whole 4x4x8 slice. The times are simulated.
256 devices in a mesh: dp: 2 (over z_lo), seq: 32 (over y, x, core), head: 4 (over z_hi).
Axes of the slice: x: 4, y: 4, z: 8 (z_hi: 4, z_lo: 2; z = z_hi * 2 + z_lo), core: 2. Of those that a mesh axis runs over, the one named last changes fastest.
Arguments:
- query_rows: bfloat16 [2, 8192, 4096], P('dp', 'seq', 'head'), may hold values from -0.59765625 to 0.59765625
- key_rows: bfloat16 [2, 8192, 4096], P('dp', 'seq', 'head'), may hold values from -0.59765625 to 0.59765625
- value_rows: bfloat16 [2, 8192, 4096], P('dp', 'seq', 'head'), may hold values from -1536 to 1536
- grad_out: bfloat16 [2, 8192, 6144], P('dp', 'seq'), may hold values from -6 to 6
- out_weight: bfloat16 [6144, 4096], P('seq', 'head'), may hold values from -0.09375 to 0.09375
- decay_rates: float32 [32], P('head'), may hold values from 0 to 1, as said below
- doc_blocks: int32 [2, 64], P('dp'), may hold values from 0 to 7, never falling along the last dimension, each value on 1 to 32 neighbouring positions
Outputs:
- grad_query: bfloat16 [2, 8192, 4096], P('dp', 'seq', 'head')
- grad_key: bfloat16 [2, 8192, 4096], P('dp', 'seq', 'head')
- grad_value: bfloat16 [2, 8192, 4096], P('dp', 'seq', 'head')
- grad_weight: float32 [6144, 4096], P('seq', 'head')
Inputs may be any that keep to these rules, and one draw needn't show every extreme that they name: `doc_blocks`: in each pack document numbers never fall from block to block; every document covers 1 to 32 blocks, and one covers exactly 32. `decay_rates`: rates are positive.
All inputs are finite; a program needn't handle non-finite values.
Results may differ from a plain program's by a relative error of at most 0.024.
Values may be sent and summed in bfloat16 or wider, within the bound.
No kernel may reach another device: no remote copies, remote signals or barrier semaphores. Data moves between devices by JAX's collectives and lax.ppermute only.
A program may use at most 192 MiB of HBM per device.

v0:
```python
import jax
import jax.numpy as jnp
from jax import lax
from jax.sharding import PartitionSpec as P

BLOCK = 128
EPSILON = 1e-05


def prefix(array, axis, join, neutral, backward):
    count = lax.axis_size(axis)
    place = lax.axis_index(axis)
    ahead = count - 1 - place if backward else place
    gathered = jax.tree.map(
        lambda a, kind: lax.all_gather(a.astype(kind), axis), array, (jnp.bfloat16, jnp.bfloat16)
    )
    state = jax.tree.map(lambda a, e: jnp.zeros_like(a) + jnp.asarray(e, a.dtype), array, neutral)

    def one(step, state):
        source = count - 1 - step if backward else step
        return join(
            state,
            jax.tree.map(
                lambda a, own: lax.dynamic_index_in_dim(a, source, 0, False).astype(own.dtype),
                gathered,
                array,
            ),
        )

    return lax.fori_loop(0, ahead, one, state)


def block_docs(doc_row, first_block, block_count, block_len):
    blocks = lax.dynamic_slice_in_dim(doc_row, first_block, block_count)
    return jnp.reshape(
        jnp.broadcast_to(blocks[:, None], (block_count, block_len)), (block_count * block_len,)
    )


def decay_masks(token_docs, decay_rates, prev_doc, next_doc):
    length = token_docs.shape[0]
    position = jnp.arange(length).astype(jnp.float32)
    rates = decay_rates[:, None]
    distance = position[:, None] - position[None, :]
    allowed = jnp.logical_and(distance >= 0, token_docs[:, None] == token_docs[None, :])
    intra = jnp.where(
        allowed[None], jnp.exp(-rates[:, :, None] * jnp.maximum(distance, 0.0)[None]), 0.0
    )
    weight_end = jnp.where(
        (token_docs == token_docs[length - 1])[None],
        jnp.exp(-rates * (length - 1.0 - position)[None]),
        0.0,
    )
    weight_start = jnp.where(
        (token_docs == token_docs[0])[None], jnp.exp(-rates * position[None]), 0.0
    )
    weight_before = jnp.where(
        (token_docs == prev_doc)[None], jnp.exp(-rates * (position + 1.0)[None]), 0.0
    )
    weight_after = jnp.where(
        (token_docs == next_doc)[None], jnp.exp(-rates * (length - position)[None]), 0.0
    )
    span_decay = jnp.exp(-decay_rates * float(length))
    link_fwd = jnp.where(token_docs[length - 1] == prev_doc, span_decay, 0.0)
    link_rev = jnp.where(token_docs[0] == next_doc, span_decay, 0.0)
    return (intra, weight_end, weight_start, weight_before, weight_after, link_fwd, link_rev)


def combine_states(earlier, later):
    return (earlier[0] * later[0], later[0][:, None, None] * earlier[1] + later[1])


def local_state(keys_here, values_here, weight_end):
    weighted = (keys_here.astype(jnp.float32) * weight_end.T[:, :, None]).astype(jnp.bfloat16)
    return jnp.einsum("jhd,jhe->hde", weighted, values_here, preferred_element_type=jnp.float32)


def forward_out(queries, keys_here, values_here, intra, weight_before, state_in):
    scores = jnp.einsum("thd,jhd->htj", queries, keys_here, preferred_element_type=jnp.float32)
    attention = (scores * intra).astype(jnp.bfloat16)
    state_low = state_in.astype(jnp.bfloat16)
    carried = jnp.einsum("thd,hde->the", queries, state_low, preferred_element_type=jnp.float32)
    output = (
        jnp.einsum("htj,jhe->the", attention, values_here, preferred_element_type=jnp.float32)
        + weight_before.T[:, :, None] * carried
    )
    inverse_rms = lax.rsqrt(jnp.mean(output * output, axis=-1, keepdims=True) + EPSILON)
    return (attention, state_low, output * inverse_rms, inverse_rms)


def backward_local(queries, values_here, intra, normal, inverse_rms, grad_normed, weight_start):
    inner = jnp.mean(grad_normed * normal, axis=-1, keepdims=True)
    grad_attn = (inverse_rms * (grad_normed - normal * inner)).astype(jnp.bfloat16)
    grad_scores = (
        jnp.einsum("the,jhe->htj", grad_attn, values_here, preferred_element_type=jnp.float32)
        * intra
    ).astype(jnp.bfloat16)
    weighted = (queries.astype(jnp.float32) * weight_start.T[:, :, None]).astype(jnp.bfloat16)
    back_local = jnp.einsum("thd,the->hde", weighted, grad_attn, preferred_element_type=jnp.float32)
    return (grad_attn, grad_scores, back_local)


def backward_rest(
    queries,
    keys_here,
    values_here,
    attention,
    state_low,
    grad_attn,
    grad_scores,
    weight_before,
    weight_after,
    state_back,
):
    back_low = state_back.astype(jnp.bfloat16)
    grad_query = jnp.einsum(
        "htj,jhd->thd", grad_scores, keys_here, preferred_element_type=jnp.float32
    ) + weight_before.T[:, :, None] * jnp.einsum(
        "the,hde->thd", grad_attn, state_low, preferred_element_type=jnp.float32
    )
    grad_key = jnp.einsum(
        "htj,thd->jhd", grad_scores, queries, preferred_element_type=jnp.float32
    ) + weight_after.T[:, :, None] * jnp.einsum(
        "jhe,hde->jhd", values_here, back_low, preferred_element_type=jnp.float32
    )
    grad_value = jnp.einsum(
        "htj,the->jhe", attention, grad_attn, preferred_element_type=jnp.float32
    ) + weight_after.T[:, :, None] * jnp.einsum(
        "jhd,hde->jhe", keys_here, back_low, preferred_element_type=jnp.float32
    )
    return (
        grad_query.astype(jnp.bfloat16),
        grad_key.astype(jnp.bfloat16),
        grad_value.astype(jnp.bfloat16),
    )


def local(query_rows, key_rows, value_rows, grad_out, out_weight, decay_rates, doc_blocks):
    tok_count = query_rows.shape[1]
    heads_here = decay_rates.shape[0]
    head_dim = query_rows.shape[2] // heads_here
    seq_count = lax.axis_size("seq")
    span_index = lax.axis_index("seq")
    block_count = tok_count // BLOCK
    total_blocks = doc_blocks.shape[1]
    queries = query_rows[0].reshape(tok_count, heads_here, head_dim)
    keys_here = key_rows[0].reshape(tok_count, heads_here, head_dim)
    values_here = value_rows[0].reshape(tok_count, heads_here, head_dim)
    grad_rows = grad_out[0]
    doc_row = doc_blocks[0]
    first_block = span_index * block_count
    token_docs = block_docs(doc_row, first_block, block_count, BLOCK)
    prev_doc = doc_row[jnp.maximum(first_block - 1, 0)]
    next_doc = doc_row[jnp.minimum(first_block + block_count, total_blocks - 1)]
    intra, weight_end, weight_start, weight_before, weight_after, link_fwd, link_rev = decay_masks(
        token_docs, decay_rates, prev_doc, next_doc
    )
    state_local = local_state(keys_here, values_here, weight_end)
    identity = (jnp.ones_like(link_fwd), jnp.zeros_like(state_local))
    state_in = prefix((link_fwd, state_local), "seq", combine_states, identity, False)[1]
    attention, state_low, normal, inverse_rms = forward_out(
        queries, keys_here, values_here, intra, weight_before, state_in
    )
    columns = grad_rows
    grad_normed = jnp.dot(
        columns,
        lax.all_gather(out_weight, "seq", axis=0, tiled=True),
        preferred_element_type=jnp.float32,
    )
    normed = normal.astype(jnp.bfloat16).reshape(tok_count, heads_here * head_dim)
    columns = grad_rows
    part = lax.dot_general(
        columns, normed, (((0,), (0,)), ((), ())), preferred_element_type=jnp.float32
    )
    weight_part = lax.psum_scatter(
        part.astype(jnp.bfloat16).astype(jnp.float32).astype(jnp.bfloat16),
        "seq",
        scatter_dimension=0,
        tiled=True,
    )
    norm_factor = (lax.axis_size("dp") * seq_count * tok_count) ** (-0.5)
    grad_weight = lax.psum(weight_part, "dp").astype(jnp.float32) * norm_factor
    grad_attn, grad_scores, back_local = backward_local(
        queries,
        values_here,
        intra,
        normal,
        inverse_rms,
        grad_normed.reshape(tok_count, heads_here, head_dim),
        weight_start,
    )
    back_identity = (jnp.ones_like(link_rev), jnp.zeros_like(back_local))
    state_back = prefix((link_rev, back_local), "seq", combine_states, back_identity, True)[1]
    grad_query, grad_key, grad_value = backward_rest(
        queries,
        keys_here,
        values_here,
        attention,
        state_low,
        grad_attn,
        grad_scores,
        weight_before,
        weight_after,
        state_back,
    )
    flat_shape = (1, tok_count, heads_here * head_dim)
    return (
        grad_query.reshape(flat_shape),
        grad_key.reshape(flat_shape),
        grad_value.reshape(flat_shape),
        grad_weight,
    )


def solution(mesh):
    in_specs = (
        P("dp", "seq", "head"),
        P("dp", "seq", "head"),
        P("dp", "seq", "head"),
        P("dp", "seq", None),
        P("seq", "head"),
        P("head"),
        P("dp", None),
    )
    out_specs = (
        P("dp", "seq", "head"),
        P("dp", "seq", "head"),
        P("dp", "seq", "head"),
        P("seq", "head"),
    )
    return jax.shard_map(local, mesh=mesh, in_specs=in_specs, out_specs=out_specs, check_vma=False)
```

profile of v0, /device:TPU:1, one launch (start us, length us, event | category | flops | bytes accessed | tf_op | source)
XLA Modules:
  0.0 419.0 jit_solution(4983138501228653416)
XLA Ops:
  8.8 1.3 constant_dynamic-slice_fusion
  12.7 2.7 bitcast_compare_fusion.3
  15.4 1.9 copy.85
  17.3 2.1 copy.58
  19.5 1.1 copy.86
  21.4 2.0 convolution_convert_fusion.1
  26.0 66.1 %all-reduce.2 = (bf16[256]{0:T(256)(128)(2,1)S(1)}, bf16[256]{0:T(256)(128)(2,1)S(1)}) all-reduce(bf16[256]{0:T(256)(128)(2,1)S(1)} %dynamic-update-slice, bf16[256]{0:T(256)(128)(2,1)S(1)} %dynamic-update-slice.1), channel_id=2, replica_groups=mesh['dp'=2,'seq'=32,'head'=4] {'seq'}, use_global_device_ids=true, to_apply=%add | all-reduce | flops 512 | bytes 2048
  92.1 2.1 copy.84
  94.4 1.9 multiply_convert_fusion.1
  97.3 1.5 convolution_bitcast_fusion.7
  99.7 2.1 while.26
  99.7 2.1 convert_add_fusion.4
  101.8 3.0 multiply_reduce_fusion.1
  104.7 51.4 %all-gather.8.cloned.1.call-done = bf16[6144,1024]{1,0:T(8,128)(2,1)} async-done(((bf16[192,1024]{1,0:T(8,128)(2,1)}), bf16[6144,1024]{1,0:T(8,128)(2,1)}) %all-gather.8.cloned.1.call-update) | async-done | bytes 12582928 | tf_op jit(solution)/shard_map/all_gather | solution.py:167
  156.1 16.7 %copy.62 = bf16[1024,6144]{1,0:T(8,128)(2,1)} copy(bf16[1024,6144]{0,1:T(8,128)(2,1)} %bitcast.111) | data formatting | bytes 25165824 | tf_op jit(solution)/shard_map/dot_general | solution.py:165
  172.8 7.0 %multiply_reduce_fusion = (f32[256,8]{0,1:T(8,128)S(1)}, f32[256,8,128]{0,2,1:T(8,128)S(1)}) fusion(f32[256,8,128]{0,2,1:T(8,128)} %get-tuple-element.186, f32[256,8]{0,1:T(8,128)S(1)} %add_rsqrt_fusion, bf16[8,128,6144]{2,1,0:T(8,128)(2,1)} %bitcast.112, bf16[1,256,6144]{2,1,0:T(8,128)(2,1)S(1)} %copy-done), kind=kOutput, calls=%fused_computation.35 | convolution fusion | flops 3222009856 | bytes 17842176 | tf_op jit(solution)/shard_map/dot_general | solution.py:165
  182.8 7.4 %convert_bitcast_fusion = bf16[6144,1024]{0,1:T(8,128)(2,1)} fusion(bf16[256,1024]{0,1:T(8,128)(2,1)} %bitcast.127, bf16[1,256,6144]{2,1,0:T(8,128)(2,1)S(1)} %copy-done), kind=kOutput, calls=%fused_computation.4 | convolution fusion | flops 3227516928 | bytes 16252928 | tf_op jit(solution)/shard_map/dot_general | solution.py:172
  190.2 16.7 %copy.82 = bf16[6144,1024]{1,0:T(8,128)(2,1)} copy(bf16[6144,1024]{0,1:T(8,128)(2,1)} %convert_bitcast_fusion) | data formatting | bytes 25165824
  210.8 1.3 convolution_bitcast_fusion.5
  212.1 1.3 convolution_bitcast_fusion.4
  213.4 37.4 %all-gather.12.cloned.1.call-done = bf16[256,128,128]{2,1,0:T(8,128)(2,1)} async-done(((bf16[8,128,128]{2,1,0:T(8,128)(2,1)}), bf16[256,128,128]{2,1,0:T(8,128)(2,1)}) %all-gather.12.cloned.1.call-update) | async-done | bytes 8388624 | tf_op jit(solution)/shard_map/all_gather | solution.py:15
  250.9 35.0 %while.27 = (s32[]{:T(128)}, f32[8,128,128]{2,1,0:T(8,128)S(1)}, s32[]{:T(128)}, bf16[32,8]{1,0:T(8,128)(2,1)S(1)}, bf16[32,8,128,128]{3,2,1,0:T(8,128)(2,1)}, /*index=5*/s32[]{:T(128)}, s32[]{:T(128)}, s32[]{:T(128)}, s32[]{:T(128)}) while((s32[]{:T(128)}, f32[8,128,128]{2,1,0:T(8,128)S(1)}, s32[]{:T(128)}, bf16[32,8]{1,0:T(8,128)(2,1)S(1)}, ...), condition=%wide.region_5.6_spmd, body=%wide.region_4.5_spmd.sunk | while | flops 393230 | bytes 1310955 | solution.py:30
  250.9 1.2 convert_add_fusion.5
  267.1 1.1 convert_add_fusion.5
  268.3 1.1 convert_add_fusion.5
  269.5 1.1 convert_add_fusion.5
  270.6 1.1 convert_add_fusion.5
  271.8 1.1 convert_add_fusion.5
  273.0 1.2 convert_add_fusion.5
  274.2 1.1 convert_add_fusion.5
  275.3 1.1 convert_add_fusion.5
  276.5 1.2 convert_add_fusion.5
  277.7 1.1 convert_add_fusion.5
  278.9 1.1 convert_add_fusion.5
  280.0 1.1 convert_add_fusion.5
  281.2 1.1 convert_add_fusion.5
  282.4 1.1 convert_add_fusion.5
  283.5 1.1 convert_add_fusion.5
  284.7 1.2 convert_add_fusion.5
  285.9 79.1 %reduce-scatter.4.cloned.1.call-done = bf16[192,1024]{1,0:T(8,128)(2,1)} async-done(((bf16[6144,1024]{1,0:T(8,128)(2,1)}), bf16[192,1024]{1,0:T(8,128)(2,1)}) %reduce-scatter.4.cloned.1.call-update) | async-done | bytes 393232
  364.9 2.0 copy.83
  367.0 1.1 fusion.13
  368.1 2.2 copy.75
  370.3 2.7 fusion.12
  373.0 2.0 copy.74
  375.0 32.9 %all-reduce.5.cloned.1.call-done = bf16[192,1024]{0,1:T(8,128)(2,1)} async-done(((bf16[192,1024]{0,1:T(8,128)(2,1)}), bf16[192,1024]{0,1:T(8,128)(2,1)}) %all-reduce.5.cloned.1.call-update) | async-done | bytes 393232 | tf_op jit(solution)/shard_map/psum | solution.py:182
  408.0 2.1 convert_multiply_fusion
  410.0 2.4 copy.76
  (124 shorter events, 28.0 us)
Async XLA Ops:
  7.2 165.6 %copy-start = (bf16[1,256,6144]{2,1,0:T(8,128)(2,1)S(1)}, bf16[1,256,6144]{2,1,0:T(8,128)(2,1)}, u32[]{:S(2)}) copy-start(bf16[1,256,6144]{2,1,0:T(8,128)(2,1)} %param.14) | copy-start | bytes 9437188
  7.2 17.1 %copy-start.20 = (u32[256]{0:T(256)S(1)}, u32[256]{0:T(256)}, u32[]{:S(2)}) copy-start(u32[256]{0:T(256)} %constant.96) | copy-start | bytes 3076
  7.2 13.4 %copy-start.19 = (f32[8]{0:T(128)S(1)}, f32[8]{0:T(128)}, u32[]{:S(2)}) copy-start(f32[8]{0:T(128)} %param.16) | copy-start | bytes 100
  7.2 91.6 %all-gather.10.cloned.1.call-start = ((), (), s32[]{:S(2)}) async-start(), calls=%async_computation.3 | async-start | bytes 8650752 | tf_op jit(solution)/shard_map/all_gather | solution.py:15
  20.6 0.8 copy-start.8
  23.5 132.6 %all-gather.8.cloned.1.call-start = ((), (), s32[]{:S(2)}) async-start(), calls=%async_computation.1 | async-start | bytes 12976128 | tf_op jit(solution)/shard_map/all_gather | solution.py:167
  24.2 226.6 %all-gather.12.cloned.1.call-start = ((), (), s32[]{:S(2)}) async-start(), calls=%async_computation.4 | async-start | bytes 8650752 | tf_op jit(solution)/shard_map/all_gather | solution.py:15
  94.2 3.1 copy-start.9
  96.3 1.0 copy-start.13
  172.8 7.0 %copy-start.12 = (f32[256,8,128]{0,2,1:T(8,128)S(1)}, f32[256,8,128]{0,2,1:T(8,128)}, u32[]{:S(2)}) copy-start(f32[256,8,128]{0,2,1:T(8,128)} %get-tuple-element.186) | copy-start | bytes 3145732
  179.8 1.9 copy-start.6
  180.9 0.8 copy-start.4
  182.7 182.2 %reduce-scatter.4.cloned.1.call-start = ((), (), s32[]{:S(2)}) async-start(), calls=%async_computation.5 | async-start | bytes 12976128
  206.9 1.0 copy-start.5
  206.9 1.2 copy-start.10
  206.9 1.9 copy-start.18
  207.0 201.0 %all-reduce.5.cloned.1.call-start = ((), (), s32[]{:S(2)}) async-start(), calls=%async_computation.2 | async-start | bytes 1048576 | tf_op jit(solution)/shard_map/psum | solution.py:182
  208.1 1.2 copy-start.3
  208.8 1.0 copy-start.16
  208.8 2.0 copy-start.14
  209.3 2.8 copy-start.7
  210.8 1.3 copy-start.17
  250.9 116.1 %copy-start.11 = (bf16[32,8,8,128]{3,2,1,0:T(8,128)(2,1)S(1)}, bf16[32,8,8,128]{3,2,1,0:T(8,128)(2,1)}, u32[]{:S(2)}) copy-start(bf16[32,8,8,128]{3,2,1,0:T(8,128)(2,1)} %copy.85) | copy-start | bytes 1572868
  250.9 116.1 %copy-start.15 = (f32[256,8,128]{0,2,1:T(8,128)S(1)}, f32[256,8,128]{0,2,1:T(8,128)}, u32[]{:S(2)}) copy-start(f32[256,8,128]{0,2,1:T(8,128)} %convolution_bitcast_fusion.5) | copy-start | bytes 3145732
  285.9 81.1 %copy-start.2 = (f32[8,128,128]{2,1,0:T(8,128)}, f32[8,128,128]{2,1,0:T(8,128)S(1)}, u32[]{:S(2)}) copy-start(f32[8,128,128]{2,1,0:T(8,128)S(1)} %get-tuple-element.133) | copy-start | bytes 1572868
  368.1 44.3 %copy-start.1 = (bf16[1,256,6144]{2,1,0:T(8,128)(2,1)S(1)}, bf16[1,256,6144]{2,1,0:T(8,128)(2,1)}, u32[]{:S(2)}) copy-start(bf16[1,256,6144]{2,1,0:T(8,128)(2,1)} %param.14) | copy-start | bytes 9437188
Sparse Core Ops, SparseCore 0:
  23.6 62.5 all-gather.9
  88.7 67.3 all-gather.7
  182.9 67.9 all-gather.11
  254.8 110.0 reduce-scatter.3
  367.6 40.3 all-reduce.4
where the time goes:
time: 422 us; the launch traced here: 419 us
  waiting for transfers between devices  201 us (48%)
  blocking collectives  66.1 us (16%)
  local copies, waits for them, and re-layouts  59 us (14%)
  other arithmetic  42.3 us (10%)
  matrix products  31.7 us (8%)
  between operations  17.3 us (4%)
    unnamed x6, waiting for transfers between devices  79.8 us
    unnamed x1, blocking collectives  66.1 us
    all_gather x1, waiting for transfers between devices, local(): lax.all_gather(out_weight, 'seq', axis=0, tiled=True)  51.4 us
    all_gather x2, waiting for transfers between devices, prefix(): lax.all_gather(a.astype(kind), axis)  37.4 us
    add x31, other arithmetic, combine_states(): later[0][:, None, None] * earlier[1] + later[1]  35.8 us
    unnamed x55, local copies, waits for them, and re-layouts  34.2 us
    psum x1, waiting for transfers between devices, local(): grad_weight = lax.psum(weight_part, 'dp').astype(jnp.float32) * norm_factor  32.9 us
    dot_general x1, local copies, waits for them, and re-layouts, local(): jnp.dot(columns, lax.all_gather(out_weight, 'seq', axis=0, tiled=True), p...  16.7 us
  transfers between devices with their start and end apart: 5, of which 4 were waited for; matrix products, arithmetic and copies ran while one was open for 20% of the time, Pallas kernels for 0%

commit v1 on v0

--- a/solution.py
+++ b/solution.py
@@ -164,7 +164,9 @@
     columns = grad_rows
     grad_normed = jnp.dot(
         columns,
-        lax.all_gather(out_weight, "seq", axis=0, tiled=True),
+        jnp.concatenate(
+            lax.all_to_all(jnp.stack([out_weight] * lax.axis_size("seq")), "seq", 0, 0), axis=0
+        ),
         preferred_element_type=jnp.float32,
     )
     normed = normal.astype(jnp.bfloat16).reshape(tok_count, heads_here * head_dim)

time: 422 us -> 594 us (1.41)
  blocking collectives: 66.1 us -> 223 us
  waiting for transfers between devices: 201 us -> 163 us
  other arithmetic: 42.3 us -> 75.3 us
  starting transfers between devices: 0.2 us -> 8.99 us
  local copies, waits for them, and re-layouts: 59 us -> 66.9 us
    unnamed x1, blocking collectives: 66.1 us -> 223 us
    all_gather x1 -> x0, waiting for transfers between devices: 51.4 us -> none  [local(): lax.all_gather(out_weight, 'seq', axis=0, tiled=True)]
    all_gather x2, waiting for transfers between devices: 37.4 us -> 81.3 us  [prefix(): lax.all_gather(a.astype(kind), axis)]
    unnamed x6 -> x5, waiting for transfers between devices: 79.8 us -> 50.6 us
    add x31, other arithmetic: 35.8 us -> 64.7 us  [combine_states(): later[0][:, None, None] * earlier[1] + later[1]]
    all_to_all x0 -> x1, starting transfers between devices: none -> 8.65 us  [local(): lax.all_to_all(jnp.stack([out_weight] * lax.axis_size('seq')), 'seq', 0, 0)]
    another operation x2 -> x3, local copies, waits for them, and re-layouts: 0.87 us -> 7.84 us  [the longest x1 6.13 us: local(): jnp.stack([out_weight] * lax.axis_size('seq'))]
  transfers between devices with their start and end apart: 5 -> 5, of which waited for: 4 -> 3; matrix products, arithmetic and copies ran while one was open for 20% -> 23% of each run, Pallas kernels for 0% -> 0%
where the time goes in v1:
time: 594 us; the launch traced here: 591 us
  blocking collectives  223 us (38%)
  waiting for transfers between devices  163 us (27%)
  other arithmetic  75.3 us (13%)
  local copies, waits for them, and re-layouts  66.9 us (11%)
  matrix products  36.7 us (6%)
  between operations  17.4 us (3%)
  starting transfers between devices  8.99 us (2%)
    unnamed x1, blocking collectives  223 us
    all_gather x2, waiting for transfers between devices, prefix(): lax.all_gather(a.astype(kind), axis)  81.3 us
    add x31, other arithmetic, combine_states(): later[0][:, None, None] * earlier[1] + later[1]  64.7 us
    unnamed x5, waiting for transfers between devices  50.6 us
    unnamed x55, local copies, waits for them, and re-layouts  35.2 us
    psum x1, waiting for transfers between devices, local(): grad_weight = lax.psum(weight_part, 'dp').astype(jnp.float32) * norm_factor  31.5 us
    dot_general x1, local copies, waits for them, and re-layouts, local(): jnp.dot(columns, jnp.concatenate(lax.all_to_all(jnp.stack([out_weight] *...  16.7 us
  transfers between devices with their start and end apart: 5, of which 3 were waited for; matrix products, arithmetic and copies ran while one was open for 23% of the time, Pallas kernels for 0%

profile of v1, /device:TPU:1, one launch (start us, length us, event | category | flops | bytes accessed | tf_op | source)
XLA Modules:
  0.0 591.1 jit_solution(8578618005997165564)
XLA Ops:
  13.8 3.3 bitcast_compare_fusion.3
  22.0 2.1 copy.58
  26.7 2.2 convolution_convert_fusion.1
  28.9 6.1 %stack.2 = bf16[32,192,1024]{2,1,0:T(8,128)(2,1)} broadcast(bf16[192,1024]{1,0:T(8,128)(2,1)S(1)} %copy-done.10), dimensions={1,2} | broadcast | bytes 12976128 | tf_op jit(solution)/shard_map/stack | solution.py:168
  35.1 8.6 %all-to-all-start = ((bf16[32,192,1024]{2,1,0:T(8,128)(2,1)}), bf16[32,192,1024]{2,1,0:T(8,128)(2,1)}, u32[]{:S(2)}, u32[]{:S(2)}) async-start(bf16[32,192,1024]{2,1,0:T(8,128)(2,1)} %stack.2), calls=%async_computation | async-start | bytes 25165824 | tf_op jit(solution)/shard_map/all_to_all | solution.py:168
  43.8 2.1 copy.84
  47.7 222.6 %all-reduce.2 = (bf16[256]{0:T(256)(128)(2,1)S(1)}, bf16[256]{0:T(256)(128)(2,1)S(1)}) all-reduce(bf16[256]{0:T(256)(128)(2,1)S(1)} %dynamic-update-slice, bf16[256]{0:T(256)(128)(2,1)S(1)} %dynamic-update-slice.1), channel_id=2, replica_groups=mesh['dp'=2,'seq'=32,'head'=4] {'seq'}, use_global_device_ids=true, to_apply=%add | all-reduce | flops 512 | bytes 2048
  275.0 16.7 %copy.62 = bf16[1024,6144]{1,0:T(8,128)(2,1)} copy(bf16[1024,6144]{0,1:T(8,128)(2,1)} %bitcast.15) | data formatting | bytes 25165824 | tf_op jit(solution)/shard_map/dot_general | solution.py:165
  296.5 6.7 %multiply_reduce_fusion = (f32[256,8]{0,1:T(8,128)S(1)}, f32[256,8,128]{0,2,1:T(8,128)S(1)}) fusion(f32[256,8,128]{0,2,1:T(8,128)S(1)} %get-tuple-element.186, f32[256,8]{0,1:T(8,128)S(1)} %add_rsqrt_fusion, bf16[8,128,6144]{2,1,0:T(8,128)(2,1)} %bitcast.113, bf16[1,256,6144]{2,1,0:T(8,128)(2,1)S(1)} %copy-done), kind=kOutput, calls=%fused_computation.35 | convolution fusion | flops 3222009856 | bytes 17842176 | tf_op jit(solution)/shard_map/dot_general | solution.py:165
  306.2 7.5 %convert_bitcast_fusion = bf16[6144,1024]{0,1:T(8,128)(2,1)} fusion(bf16[256,1024]{0,1:T(8,128)(2,1)} %bitcast.128, bf16[1,256,6144]{2,1,0:T(8,128)(2,1)S(1)} %copy-done), kind=kOutput, calls=%fused_computation.4 | convolution fusion | flops 3227516928 | bytes 16252928 | tf_op jit(solution)/shard_map/dot_general | solution.py:174
  313.7 16.7 %copy.82 = bf16[6144,1024]{1,0:T(8,128)(2,1)} copy(bf16[6144,1024]{0,1:T(8,128)(2,1)} %convert_bitcast_fusion) | data formatting | bytes 25165824
  336.4 2.8 convolution_bitcast_fusion.5
  339.2 2.3 convolution_bitcast_fusion.4
  341.5 81.3 %all-gather.9.cloned.1.call-done = bf16[256,128,128]{2,1,0:T(8,128)(2,1)} async-done(((bf16[8,128,128]{2,1,0:T(8,128)(2,1)}), bf16[256,128,128]{2,1,0:T(8,128)(2,1)}) %all-gather.9.cloned.1.call-update) | async-done | bytes 8388624 | tf_op jit(solution)/shard_map/all_gather | solution.py:15
  423.7 62.9 %while.27 = (s32[]{:T(128)}, f32[8,128,128]{2,1,0:T(8,128)}, s32[]{:T(128)}, bf16[32,8]{1,0:T(8,128)(2,1)S(1)}, bf16[32,8,128,128]{3,2,1,0:T(8,128)(2,1)}, /*index=5*/s32[]{:T(128)}, s32[]{:T(128)}, s32[]{:T(128)}, s32[]{:T(128)}) while((s32[]{:T(128)}, f32[8,128,128]{2,1,0:T(8,128)}, s32[]{:T(128)}, bf16[32,8]{1,0:T(8,128)(2,1)S(1)}, ...), condition=%wide.region_5.6_spmd, body=%wide.region_4.5_spmd.sunk | while | flops 393230 | bytes 1310947 | solution.py:30
  425.8 2.1 convert_add_fusion.5
  427.8 2.1 convert_add_fusion.5
  429.9 2.1 convert_add_fusion.5
  432.0 2.1 convert_add_fusion.5
  434.0 2.1 convert_add_fusion.5
  436.1 2.1 convert_add_fusion.5
  438.2 2.1 convert_add_fusion.5
  440.3 2.1 convert_add_fusion.5
  442.4 2.1 convert_add_fusion.5
  444.6 2.1 convert_add_fusion.5
  446.7 2.1 convert_add_fusion.5
  448.8 2.1 convert_add_fusion.5
  450.9 2.1 convert_add_fusion.5
  453.0 2.1 convert_add_fusion.5
  455.1 2.1 convert_add_fusion.5
  457.3 2.1 convert_add_fusion.5
  459.4 2.1 convert_add_fusion.5
  461.5 2.1 convert_add_fusion.5
  463.7 2.1 convert_add_fusion.5
  465.8 2.1 convert_add_fusion.5
  467.9 2.1 convert_add_fusion.5
  470.0 2.1 convert_add_fusion.5
  472.0 2.1 convert_add_fusion.5
  474.1 2.1 convert_add_fusion.5
  476.2 2.1 convert_add_fusion.5
  482.4 2.1 convert_add_fusion.5
  484.5 2.1 convert_add_fusion.5
  486.6 50.5 %reduce-scatter.4.cloned.1.call-done = bf16[192,1024]{1,0:T(8,128)(2,1)} async-done(((bf16[6144,1024]{1,0:T(8,128)(2,1)}), bf16[192,1024]{1,0:T(8,128)(2,1)}) %reduce-scatter.4.cloned.1.call-update) | async-done | bytes 393232
  539.1 2.7 fusion.13
  543.9 2.7 fusion.12
  548.6 31.5 %all-reduce.5.cloned.1.call-done = bf16[192,1024]{0,1:T(8,128)(2,1)} async-done(((bf16[192,1024]{0,1:T(8,128)(2,1)}), bf16[192,1024]{0,1:T(8,128)(2,1)}) %all-reduce.5.cloned.1.call-update) | async-done | bytes 393232 | tf_op jit(solution)/shard_map/psum | solution.py:184
  580.1 2.1 convert_multiply_fusion
  582.2 2.4 copy.76
  (124 shorter events, 46.5 us)
Async XLA Ops:
  7.2 289.4 %copy-start = (bf16[1,256,6144]{2,1,0:T(8,128)(2,1)S(1)}, bf16[1,256,6144]{2,1,0:T(8,128)(2,1)}, u32[]{:S(2)}) copy-start(bf16[1,256,6144]{2,1,0:T(8,128)(2,1)} %param.14) | copy-start | bytes 9437188
  7.2 17.0 %copy-start.17 = (f32[8]{0:T(128)S(1)}, f32[8]{0:T(128)}, u32[]{:S(2)}) copy-start(f32[8]{0:T(128)} %param.16) | copy-start | bytes 100
  7.2 21.7 %copy-start.10 = (bf16[192,1024]{1,0:T(8,128)(2,1)S(1)}, bf16[192,1024]{1,0:T(8,128)(2,1)}, u32[]{:S(2)}) copy-start(bf16[192,1024]{1,0:T(8,128)(2,1)} %param.15) | copy-start | bytes 1179652
  7.2 284.5 %all-gather.7.cloned.1.call-start = ((), (), s32[]{:S(2)}) async-start(), calls=%async_computation.3 | async-start | bytes 8650752 | tf_op jit(solution)/shard_map/all_gather | solution.py:15
  8.7 0.6 copy-start.13
  24.7 0.5 copy-start.15
  35.0 10.8 %copy-start.20 = (u32[256]{0:T(256)S(1)}, u32[256]{0:T(256)}, u32[]{:S(2)}) copy-start(u32[256]{0:T(256)} %constant.96) | copy-start | bytes 3076
  35.0 12.2 %copy-start.19 = (bf16[8]{0:T(256)(128)(2,1)S(1)}, bf16[8]{0:T(256)(128)(2,1)}, u32[]{:S(2)}) copy-start(bf16[8]{0:T(256)(128)(2,1)} %get-tuple-element.181) | copy-start | bytes 52
  35.0 12.4 %copy-start.18 = (bf16[8]{0:T(256)(128)(2,1)S(1)}, bf16[8]{0:T(256)(128)(2,1)}, u32[]{:S(2)}) copy-start(bf16[8]{0:T(256)(128)(2,1)} %get-tuple-element.180) | copy-start | bytes 52
  35.0 235.3 %copy-start.12 = (f32[256]{0:T(256)S(1)}, f32[256]{0:T(256)}, u32[]{:S(2)}) copy-start(f32[256]{0:T(256)} %iota_convert_fusion) | copy-start | bytes 3076
  35.0 235.3 %copy-start.14 = (s32[256]{0:T(256)S(1)}, s32[256]{0:T(256)}, u32[]{:S(2)}) copy-start(s32[256]{0:T(256)} %copy-done.13) | copy-start | bytes 3076
  35.1 235.6 %copy-start.16 = (f32[8]{0:T(128)S(1)}, f32[8]{0:T(128)}, u32[]{:S(2)}) copy-start(f32[8]{0:T(128)} %copy-done.15) | copy-start | bytes 100
  35.1 239.9 %all-to-all-start = ((bf16[32,192,1024]{2,1,0:T(8,128)(2,1)}), bf16[32,192,1024]{2,1,0:T(8,128)(2,1)}, u32[]{:S(2)}, u32[]{:S(2)}) async-start(bf16[32,192,1024]{2,1,0:T(8,128)(2,1)} %stack.2), calls=%async_computation | async-start | bytes 25165824 | tf_op jit(solution)/shard_map/all_to_all | solution.py:168
  43.7 379.1 %all-gather.9.cloned.1.call-start = ((), (), s32[]{:S(2)}) async-start(), calls=%async_computation.4 | async-start | bytes 8650752 | tf_op jit(solution)/shard_map/all_gather | solution.py:15
  270.4 3.2 copy-start.5
  272.6 1.0 copy-start.6
  303.2 1.9 copy-start.4
  303.2 1.9 copy-start.11
  304.3 0.8 copy-start.2
  306.1 231.0 %reduce-scatter.4.cloned.1.call-start = ((), (), s32[]{:S(2)}) async-start(), calls=%async_computation.5 | async-start | bytes 12976128
  330.4 249.7 %all-reduce.5.cloned.1.call-start = ((), (), s32[]{:S(2)}) async-start(), calls=%async_computation.2 | async-start | bytes 1048576 | tf_op jit(solution)/shard_map/psum | solution.py:184
  330.7 2.0 copy-start.9
  330.7 2.5 copy-start.1
  330.7 2.5 copy-start.3
  332.7 1.6 copy-start.7
  336.4 2.8 copy-start.8
Sparse Core Ops, SparseCore 0:
  29.0 174.9 all-gather.6
  306.3 116.5 all-gather.8
  427.0 110.0 reduce-scatter.3
  539.7 40.3 all-reduce.4
